TPU v7x, 32 devices: a whole 2x2x4 slice. The times are simulated.
32 devices in a mesh: occ: 4 (over z), pan: 8 (over y, x, core).
Axes of the slice: x: 2, y: 2, z: 4, core: 2. Of those that a mesh axis runs over, the one named last changes fastest.
Arguments:
- gamma_ia: bfloat16 [2, 1024, 8704], P(None, 'occ', 'pan'), may hold values from -6 to 6
- coef_virt: bfloat16 [10240, 8704], P(None, 'pan'), may hold values from -0.09375 to 0.09375
- coef_occ: bfloat16 [10240, 1024], P('occ'), may hold values from -0.1875 to 0.1875
- tile_mask: int32 [80, 80], replicated, may hold values from 0 to 1, as said below
- tile_owner: int32 [80, 80], replicated, may hold values from 0 to 7, as said below
Outputs:
- gradient_tiles: bfloat16 [4, 8, 8, 2, 2, 128, 128], P('occ', 'pan')
Inputs may be any that keep to these rules, and one draw needn't show every extreme that they name: `tile_mask`: each block of 20 x 10 tiles holds at most 16 ones. `tile_owner`: within each block of 20 x 10 tiles, at most 2 tiles with tile_mask 1 share an owner; in every draw some block gives exactly 2 such tiles to one owner.
All inputs are finite; a program needn't handle non-finite values.
Results may differ from a plain program's by a relative error of at most 0.005.
Values may be sent and summed in bfloat16 or wider, within the bound.
A program may use at most 128 MiB of HBM per device.

v0:
```python
import jax
import jax.numpy as jnp
from jax import lax
from jax.sharding import PartitionSpec as P

AUX = 2
TILE = 128
SCAP = 2


def route_slots(block_mask, block_owner, owners):
    usable = block_mask.reshape(-1)
    owners_of = block_owner.reshape(-1)
    belongs = (
        (usable[:, None] == 1)
        & (owners_of[:, None] == jnp.arange(owners, dtype=jnp.int32)[None, :])
    ).astype(jnp.int32)
    order_rank = jnp.cumsum(belongs, axis=0) - belongs
    matched = belongs[:, :, None] * (
        order_rank[:, :, None] == jnp.arange(SCAP, dtype=jnp.int32)[None, None, :]
    ).astype(jnp.int32)
    tile_index = jnp.arange(usable.shape[0], dtype=jnp.int32)
    slot_tile = jnp.sum(matched * tile_index[:, None, None], axis=0)
    filled = jnp.sum(matched, axis=0)
    return (slot_tile, filled)


def local(gamma_ia, coef_virt, coef_occ, tile_mask, tile_owner):
    panels = lax.axis_size("pan")
    occ_local = gamma_ia.shape[1]
    panel_width = coef_virt.shape[0] // panels
    row_width = coef_occ.shape[0]
    row_tiles = row_width // TILE
    col_tiles = panel_width // TILE
    gamma_flat = gamma_ia.reshape(AUX * occ_local, gamma_ia.shape[2])
    summed = lax.psum_scatter(
        lax.dot_general(
            coef_virt, gamma_flat, (((1,), (1,)), ((), ())), preferred_element_type=jnp.float32
        ),
        "pan",
        scatter_dimension=0,
        tiled=True,
    )
    half_x = summed.astype(jnp.bfloat16).reshape(panel_width, AUX, occ_local)
    whole_x = lax.all_gather(half_x, "occ", axis=2, tiled=True)
    row_block = lax.axis_index("occ")
    col_block = lax.axis_index("pan")
    block_mask = lax.dynamic_slice(
        tile_mask, (row_block * row_tiles, col_block * col_tiles), (row_tiles, col_tiles)
    )
    block_owner = lax.dynamic_slice(
        tile_owner, (row_block * row_tiles, col_block * col_tiles), (row_tiles, col_tiles)
    )
    slot_tile, filled = route_slots(block_mask, block_owner, panels)
    flat_slots = slot_tile.reshape(-1)
    tile_rows = flat_slots // col_tiles
    tile_cols = flat_slots % col_tiles
    row_set = jnp.take(coef_occ.reshape(row_tiles, TILE, coef_occ.shape[1]), tile_rows, axis=0)
    col_set = jnp.take(whole_x.reshape(col_tiles, TILE, AUX, whole_x.shape[2]), tile_cols, axis=0)
    picked = jnp.einsum("sri,skpi->sprk", row_set, col_set, preferred_element_type=jnp.float32)
    picked = (
        picked.reshape(panels, SCAP, AUX, TILE, TILE)
        * filled.astype(jnp.float32)[:, :, None, None, None]
    )
    arrived = lax.all_to_all(
        picked.astype(jnp.bfloat16), "pan", split_axis=0, concat_axis=0, tiled=True
    )
    return arrived[None, None]


def solution(mesh):
    return jax.shard_map(
        local,
        mesh=mesh,
        in_specs=(P(None, "occ", "pan"), P(None, "pan"), P("occ", None), P(), P()),
        out_specs=P("occ", "pan", None, None, None, None, None),
        check_vma=False,
    )
```

profile of v0, /device:TPU:1, one launch (start us, length us, event | category | flops | bytes accessed | tf_op | source)
XLA Modules:
  0.0 319.5 jit_solution(1969486776667093120)
XLA Ops:
  6.5 1.7 copy.20
  8.2 22.2 %fusion.15 = f32[10240,512]{1,0:T(8,128)} fusion(bf16[10240,1088]{0,1:T(8,128)(2,1)} %param.6, bf16[512,1088]{1,0:T(8,128)(2,1)S(1)} %bitcast.34), kind=kOutput, calls=%fused_computation.44 | convolution fusion | flops 11408506880 | bytes 44367872 | tf_op jit(solution)/shard_map/dot_general | solution.py:37
  30.4 0.2 all-gather.2.cloned.1.call-start
  30.6 138.2 %reduce-scatter.2.cloned.1.call-done = f32[1280,512]{1,0:T(8,128)} async-done(((f32[10240,512]{1,0:T(8,128)}), f32[1280,512]{1,0:T(8,128)}) %reduce-scatter.2.cloned.1.call-update) | async-done | bytes 2621456 | tf_op jit(solution)/shard_map/reduce_scatter | solution.py:36
  168.8 1.9 convert_element_type.23
  170.7 1.2 copy.33
  171.9 0.8 dynamic_slice.7
  172.7 0.1 eq.58
  172.8 0.8 dynamic-slice_compare_fusion
  173.6 0.1 eq.57
  173.8 0.6 reduce-window.6
  174.4 0.2 slice_reduce_fusion
  174.7 0.2 select_reduce_fusion
  175.1 0.1 copy.24
  175.2 0.1 ne.64
  175.8 5.2 %gather_fusion.1 = bf16[16,128,1024]{2,1,0:T(8,128)(2,1)} fusion(bf16[20,128,1024]{2,1,0:T(8,128)(2,1)} %bitcast.32, s32[1024]{0:T(1024)S(1)} %get-tuple-element.13), kind=kCustom, calls=%fused_computation.1 | custom fusion | bytes 8388672 | tf_op jit(solution)/shard_map/jit(_take)/gather | solution.py:58
  181.0 87.4 %all-gather.2.cloned.1.call-done = bf16[1280,2,1024]{2,0,1:T(8,128)(2,1)} async-done(((bf16[1280,2,256]{2,0,1:T(8,128)(2,1)}), bf16[1280,2,1024]{2,0,1:T(8,128)(2,1)}) %all-gather.2.cloned.1.call-update) | async-done | bytes 5242896 | tf_op jit(solution)/shard_map/all_gather | solution.py:45
  268.4 5.7 %copy.23 = bf16[10,128,2,1024]{3,1,2,0:T(8,128)(2,1)} copy(bf16[10,128,2,1024]{3,1,0,2:T(8,128)(2,1)} %bitcast.28) | data formatting | bytes 10485760 | tf_op jit(solution)/shard_map/reshape | solution.py:59
  274.1 7.2 %gather_fusion = bf16[16,128,2,1024]{3,1,2,0:T(8,128)(2,1)} fusion(bf16[10,128,2,1024]{3,1,2,0:T(8,128)(2,1)} %copy.23, s32[1024]{0:T(1024)S(1)} %get-tuple-element.14), kind=kCustom, calls=%fused_computation | custom fusion | bytes 16777280 | tf_op jit(solution)/shard_map/jit(_take)/gather | solution.py:59
  281.3 8.4 %fusion = f32[16,128,2,128]{3,1,2,0:T(8,128)} fusion(bf16[16,128,2,1024]{3,1,2,0:T(8,128)(2,1)} %gather_fusion, pred[16]{0:T(512)(128)(4,1)S(1)} %get-tuple-element.10, bf16[16,128,1024]{2,1,0:T(8,128)(2,1)} %gather_fusion.1, pred[16]{0:T(512)(128)(4,1)S(1)} %get-tuple-element.9), kind=kOutput, calls=%fused_computation.2 | convolution fusion | flops 1080033280 | bytes 14680096 | tf_op jit(solution)/shard_map/sri,skpi->sprk/dot_general | solution.py:60
  289.7 1.9 copy.29
  291.6 0.3 multiply_convert_fusion
  292.0 19.7 %all_to_all.5 = bf16[8,2,2,128,128]{4,3,2,1,0:T(8,128)(2,1)S(1)} all-to-all(bf16[8,2,2,128,128]{4,3,2,1,0:T(8,128)(2,1)S(1)} %multiply_convert_fusion), channel_id=1, replica_groups=mesh['occ'=4,'pan'=8] {'pan'}, dimensions={0} | all-to-all | bytes 2097152 | tf_op jit(solution)/shard_map/all_to_all | solution.py:65
  311.7 1.0 copy.35
  (24 shorter events, 0.9 us)
Async XLA Ops:
  6.5 162.3 %reduce-scatter.2.cloned.1.call-start = ((), (), s32[]{:S(2)}) async-start(), calls=%async_computation.2 | async-start | bytes 23592960 | tf_op jit(solution)/shard_map/reduce_scatter | solution.py:36
  30.4 238.0 %all-gather.2.cloned.1.call-start = ((), (), s32[]{:S(2)}) async-start(), calls=%async_computation.3 | async-start | bytes 6553600 | tf_op jit(solution)/shard_map/all_gather | solution.py:45
Sparse Core Ops, SparseCore 0:
  30.5 138.2 reduce-scatter.1
  172.1 96.3 all-gather.1
where the time goes:
time: 321 us; the launch traced here: 319 us
  waiting for transfers between devices  226 us (70%)
  matrix products  30.5 us (10%)
  local copies, waits for them, and re-layouts  25.9 us (8%)
  blocking collectives  19.7 us (6%)
  between operations  13.5 us (4%)
  other arithmetic  3.97 us (1%)
    reduce_scatter x1, waiting for transfers between devices, local(): lax.psum_scatter(lax.dot_general(coef_virt, gamma_flat, (((1,), (1,)), ((...  138 us
    all_gather x1, waiting for transfers between devices, local(): whole_x = lax.all_gather(half_x, 'occ', axis=2, tiled=True)  87.4 us
    dot_general x1, matrix products, local(): lax.dot_general(coef_virt, gamma_flat, (((1,), (1,)), ((), ())), preferre...  22.2 us
    all_to_all x1, blocking collectives, local(): lax.all_to_all(picked.astype(jnp.bfloat16), 'pan', split_axis=0, concat_a...  19.7 us
    dot_general x1, matrix products, local(): jnp.einsum('sri,skpi->sprk', row_set, col_set, preferred_element_type=jnp...  8.38 us
    gather x1, local copies, waits for them, and re-layouts, local(): jnp.take(whole_x.reshape(col_tiles, TILE, AUX, whole_x.shape[2]), tile_co...  7.21 us
  transfers between devices with their start and end apart: 2, of which 2 were waited for; matrix products, arithmetic and copies ran while one was open for 3% of the time, Pallas kernels for 0%

commit v1 on v0

v1 whole, which is shorter than its diff:
```python
import functools

import jax
import jax.numpy as jnp
from jax import lax
from jax.experimental import pallas as pl
from jax.experimental.pallas import tpu as pltpu
from jax.sharding import PartitionSpec as P

AUX = 2
TILE = 128
SCAP = 2
CHUNKS = 5
MESH = pl.DeviceIdType.MESH


def route_slots(block_mask, block_owner, owners):
    usable = block_mask.reshape(-1)
    owners_of = block_owner.reshape(-1)
    belongs = (
        (usable[:, None] == 1)
        & (owners_of[:, None] == jnp.arange(owners, dtype=jnp.int32)[None, :])
    ).astype(jnp.int32)
    order_rank = jnp.cumsum(belongs, axis=0) - belongs
    matched = belongs[:, :, None] * (
        order_rank[:, :, None] == jnp.arange(SCAP, dtype=jnp.int32)[None, None, :]
    ).astype(jnp.int32)
    tile_index = jnp.arange(usable.shape[0], dtype=jnp.int32)
    slot_tile = jnp.sum(matched * tile_index[:, None, None], axis=0)
    filled = jnp.sum(matched, axis=0)
    return (slot_tile, filled)


def block_slots(tile_mask, tile_owner, row_tiles, col_tiles, panels):
    row_block = lax.axis_index("occ")
    col_block = lax.axis_index("pan")
    corner = (row_block * row_tiles, col_block * col_tiles)
    block_mask = lax.dynamic_slice(tile_mask, corner, (row_tiles, col_tiles))
    block_owner = lax.dynamic_slice(tile_owner, corner, (row_tiles, col_tiles))
    return route_slots(block_mask, block_owner, panels)


def by_collectives(gamma_ia, coef_virt, coef_occ, tile_mask, tile_owner):
    panels = lax.axis_size("pan")
    occ_local = gamma_ia.shape[1]
    panel_width = coef_virt.shape[0] // panels
    row_tiles = coef_occ.shape[0] // TILE
    col_tiles = panel_width // TILE
    gamma_flat = gamma_ia.reshape(AUX * occ_local, gamma_ia.shape[2])
    summed = lax.psum_scatter(
        lax.dot_general(
            coef_virt, gamma_flat, (((1,), (1,)), ((), ())), preferred_element_type=jnp.float32
        ),
        "pan",
        scatter_dimension=0,
        tiled=True,
    )
    half_x = summed.astype(jnp.bfloat16).reshape(panel_width, AUX, occ_local)
    whole_x = lax.all_gather(half_x, "occ", axis=2, tiled=True)
    slot_tile, filled = block_slots(tile_mask, tile_owner, row_tiles, col_tiles, panels)
    flat_slots = slot_tile.reshape(-1)
    row_set = jnp.take(
        coef_occ.reshape(row_tiles, TILE, coef_occ.shape[1]), flat_slots // col_tiles, axis=0
    )
    col_set = jnp.take(
        whole_x.reshape(col_tiles, TILE, AUX, whole_x.shape[2]), flat_slots % col_tiles, axis=0
    )
    picked = jnp.einsum("sri,skpi->sprk", row_set, col_set, preferred_element_type=jnp.float32)
    picked = (
        picked.reshape(panels, SCAP, AUX, TILE, TILE)
        * filled.astype(jnp.float32)[:, :, None, None, None]
    )
    arrived = lax.all_to_all(
        picked.astype(jnp.bfloat16), "pan", split_axis=0, concat_axis=0, tiled=True
    )
    return arrived[None, None]


def kernel(
    n_occ, n_pan, chunks,
    rows_of, cols_of, filled_of, gamma_ref, virt_ref, occ_ref, out_ref,
    virt, coef, send_c, recv_c, keep_a, keep_b, send_a, recv_a, send_b, recv_b,
    keep_2, send_2a, recv_2a, send_2b, recv_2b, whole, picked,
    load_sem, coef_sem, own_sem,
    c_out, c_in, a_out, a_in, b_out, b_in, a2_out, a2_in, b2_out, b2_in,
    z_out, z_in, t_out, t_in,
):
    o = lax.axis_index("occ")
    s = lax.axis_index("pan")
    core = lax.rem(s, 2)
    x = lax.rem(s // 2, 2)
    y = s // 4
    other_core = s + 1 - 2 * core
    other_x = s + 2 - 4 * x
    other_y = s + 4 - 8 * y
    group = n_pan // 2
    width = virt.shape[3]
    tiles = width // TILE
    half = gamma_ref.shape[1]

    def load(q, cc):
        return pltpu.make_async_copy(
            virt_ref.at[:, cc, pl.ds(pl.multiple_of(q * width, width), width), :],
            virt.at[q, cc],
            load_sem.at[q, cc],
        )

    for q in range(chunks):
        load(q, 1 - core).start()
        load(q, core).start()
    fetch = pltpu.make_async_copy(occ_ref, coef, coef_sem)
    fetch.start()

    barrier = pltpu.get_barrier_semaphore()
    for d in range(1, n_pan):
        pl.semaphore_signal(
            barrier, inc=1, device_id=(o, lax.rem(s + d, n_pan)), device_id_type=MESH
        )
    for d in range(1, n_occ):
        pl.semaphore_signal(
            barrier, inc=1, device_id=(lax.rem(o + d, n_occ), s), device_id_type=MESH
        )
    pl.semaphore_wait(barrier, n_pan + n_occ - 2)

    def remote(src, dst, out_sem, in_sem, pan, row=None):
        return pltpu.make_async_remote_copy(
            src_ref=src, dst_ref=dst, send_sem=out_sem, recv_sem=in_sem,
            device_id=(o if row is None else row, pan), device_id_type=MESH,
        )

    def copy_c(q):
        return remote(send_c.at[q], recv_c.at[q], c_out.at[q], c_in.at[q], other_core)

    def copy_a(q):
        return remote(send_a.at[q], recv_a.at[q], a_out.at[q], a_in.at[q], other_x)

    def copy_b(q):
        return remote(send_b.at[q], recv_b.at[q], b_out.at[q], b_in.at[q], other_y)

    def copy_2a(q):
        return remote(send_2a.at[q], recv_2a.at[q], a2_out.at[q], a2_in.at[q], other_y)

    def copy_2b(q):
        return remote(send_2b.at[q], recv_2b.at[q], b2_out.at[q], b2_in.at[q], other_x)

    def copy_z(q, d, source):
        part = whole.at[source, pl.ds(q * tiles, tiles)]
        return remote(
            part, part, z_out.at[d - 1, q], z_in.at[d - 1, q], s, lax.rem(o + d, n_occ)
        )

    def product(q, cc, g):
        return lax.dot_general(
            virt[q, cc, g],
            gamma_ref[...].reshape(AUX * half, gamma_ref.shape[2]),
            (((1,), (1,)), ((), ())),
            preferred_element_type=jnp.float32,
        )

    def step(it, carry):
        @pl.when(it >= 3)
        def _():
            q = it - 3
            copy_2a(q).wait_recv()
            copy_2b(q).wait_recv()
            for p, arrived in ((0, recv_2a), (1, recv_2b)):
                total = keep_2[p] + arrived[q].astype(jnp.float32)
                total = total.astype(jnp.bfloat16)
                for t in range(tiles):
                    whole[o, q * tiles + t, p] = total[t * TILE:(t + 1) * TILE]
            for d in range(1, n_occ):
                copy_z(q, d, o).start()

        @pl.when((it >= 2) & (it < chunks + 2))
        def _():
            q = it - 2
            copy_a(q).wait_recv()
            send_2a[q] = (keep_a[1] + recv_a[q, 1].astype(jnp.float32)).astype(jnp.bfloat16)
            copy_2a(q).start()
            copy_b(q).wait_recv()
            send_2b[q] = (keep_b[1] + recv_b[q, 1].astype(jnp.float32)).astype(jnp.bfloat16)
            copy_2b(q).start()
            keep_2[0] = keep_a[0] + recv_a[q, 0].astype(jnp.float32)
            keep_2[1] = keep_b[0] + recv_b[q, 0].astype(jnp.float32)

        @pl.when((it >= 1) & (it < chunks + 1))
        def _():
            q = it - 1
            load(q, core).wait()
            copy_c(q).wait_recv()
            for b, a in ((1, 1), (0, 1), (1, 0), (0, 0)):
                gx = x + a - 2 * x * a
                gy = y + b - 2 * y * b
                g = gy * 2 + gx
                total = product(q, core, g) + recv_c[q, g].astype(jnp.float32)
                if a:
                    send_a[q, b] = total[:, :half].astype(jnp.bfloat16)
                else:
                    keep_a[b] = total[:, :half]
                if b:
                    send_b[q, a] = total[:, half:].astype(jnp.bfloat16)
                else:
                    keep_b[a] = total[:, half:]
                if (b, a) == (0, 1):
                    copy_a(q).start()
                if (b, a) == (1, 0):
                    copy_b(q).start()

        @pl.when(it < chunks)
        def _():
            load(it, 1 - core).wait()

            def one(g, c):
                send_c[it, g] = product(it, 1 - core, g).astype(jnp.bfloat16)
                return c

            lax.fori_loop(0, group, one, 0)
            copy_c(it).start()

        return carry

    lax.fori_loop(0, chunks + 3, step, 0)

    fetch.wait()
    for d in range(1, n_occ):
        def arrive(q, c, d=d):
            copy_z(q, d, lax.rem(o + n_occ - d, n_occ)).wait_recv()
            return c
        lax.fori_loop(0, chunks, arrive, 0)

    def tile_send(d):
        j = lax.rem(s + d, n_pan)
        return remote(
            picked.at[j], out_ref.at[s], t_out.at[d - 1], t_in.at[d - 1], j
        )

    def one_owner(d, c):
        j = lax.rem(s + d, n_pan)
        for k in range(SCAP):
            row = rows_of[j * SCAP + k]
            col = cols_of[j * SCAP + k]
            kept = filled_of[j * SCAP + k].astype(jnp.float32)
            total = jnp.zeros((TILE, AUX * TILE), jnp.float32)
            for z in range(n_occ):
                total += lax.dot_general(
                    coef[row, :, z * half:(z + 1) * half],
                    whole[z, col].reshape(AUX * TILE, half),
                    (((1,), (1,)), ((), ())),
                    preferred_element_type=jnp.float32,
                )
            total = (total * kept).astype(jnp.bfloat16)
            for p in range(AUX):
                picked[j, k, p] = total[:, p * TILE:(p + 1) * TILE]

        @pl.when(d < n_pan)
        def _():
            tile_send(d).start()

        return c

    lax.fori_loop(1, n_pan + 1, one_owner, 0)
    own = pltpu.make_async_copy(picked.at[s], out_ref.at[s], own_sem)
    own.start()

    def drain(q, c):
        for copy in (copy_c, copy_a, copy_b, copy_2a, copy_2b):
            copy(q).wait_send()
        for d in range(1, n_occ):
            copy_z(q, d, o).wait_send()
        return c

    lax.fori_loop(0, chunks, drain, 0)

    def finish(d, c):
        tile_send(d).wait_send()
        source = lax.rem(s + n_pan - d, n_pan)
        remote(
            picked.at[source], out_ref.at[source], t_out.at[d - 1], t_in.at[d - 1], source
        ).wait_recv()
        return c

    lax.fori_loop(1, n_pan, finish, 0)
    own.wait()


def by_kernel(n_occ, n_pan, gamma_ia, coef_virt, coef_occ, tile_mask, tile_owner):
    half = gamma_ia.shape[1]
    depth = gamma_ia.shape[2]
    panel_width = coef_virt.shape[0] // n_pan
    row_tiles = coef_occ.shape[0] // TILE
    col_tiles = panel_width // TILE
    chunks = CHUNKS if col_tiles % CHUNKS == 0 else 1
    width = panel_width // chunks
    group = n_pan // 2
    slot_tile, filled = block_slots(tile_mask, tile_owner, row_tiles, col_tiles, n_pan)
    flat_slots = slot_tile.reshape(-1)
    bf16, f32 = jnp.bfloat16, jnp.float32
    dma = pltpu.SemaphoreType.DMA
    smem = pl.BlockSpec(memory_space=pltpu.SMEM)
    hbm = pl.BlockSpec(memory_space=pl.ANY)
    arrived = pl.pallas_call(
        functools.partial(kernel, n_occ, n_pan, chunks),
        out_shape=jax.ShapeDtypeStruct((n_pan, SCAP, AUX, TILE, TILE), bf16),
        in_specs=[smem, smem, smem, pl.BlockSpec(memory_space=pltpu.VMEM), hbm, hbm],
        out_specs=hbm,
        scratch_shapes=[
            pltpu.VMEM((chunks, 2, group, width, depth), bf16),
            pltpu.VMEM((row_tiles, TILE, coef_occ.shape[1]), bf16),
            pltpu.VMEM((chunks, group, width, AUX * half), bf16),
            pltpu.VMEM((chunks, group, width, AUX * half), bf16),
            pltpu.VMEM((2, width, half), f32),
            pltpu.VMEM((2, width, half), f32),
            pltpu.VMEM((chunks, 2, width, half), bf16),
            pltpu.VMEM((chunks, 2, width, half), bf16),
            pltpu.VMEM((chunks, 2, width, half), bf16),
            pltpu.VMEM((chunks, 2, width, half), bf16),
            pltpu.VMEM((2, width, half), f32),
            pltpu.VMEM((chunks, width, half), bf16),
            pltpu.VMEM((chunks, width, half), bf16),
            pltpu.VMEM((chunks, width, half), bf16),
            pltpu.VMEM((chunks, width, half), bf16),
            pltpu.VMEM((n_occ, col_tiles, AUX, TILE, half), bf16),
            pltpu.VMEM((n_pan, SCAP, AUX, TILE, TILE), bf16),
            dma((chunks, 2)), dma, dma,
            *[dma((chunks,)) for _ in range(10)],
            dma((n_occ - 1, chunks)), dma((n_occ - 1, chunks)),
            dma((n_pan - 1,)), dma((n_pan - 1,)),
        ],
        compiler_params=pltpu.CompilerParams(
            collective_id=0, has_side_effects=True, vmem_limit_bytes=67043328
        ),
    )(
        flat_slots // col_tiles,
        flat_slots % col_tiles,
        filled.reshape(-1),
        gamma_ia,
        coef_virt.reshape(group, 2, panel_width, depth),
        coef_occ.reshape(row_tiles, TILE, coef_occ.shape[1]),
    )
    return arrived[None, None]


def solution(mesh):
    n_occ, n_pan = mesh.shape["occ"], mesh.shape["pan"]
    local = functools.partial(by_kernel, n_occ, n_pan) if n_pan == 8 else by_collectives
    return jax.shard_map(
        local,
        mesh=mesh,
        in_specs=(P(None, "occ", "pan"), P(None, "pan"), P("occ", None), P(), P()),
        out_specs=P("occ", "pan", None, None, None, None, None),
        check_vma=False,
    )
```

time: 321 us -> 190 us (0.59)
  the two profiles are of different devices: /device:TPU:1 before, /device:TPU:9 now
where the time goes in v1:
time: 190 us; the launch traced here: 189 us
  Pallas kernels  152 us (80%)
  local copies, waits for them, and re-layouts  34.6 us (18%)
  other arithmetic  2.21 us (1%)
    pallas_call x1, Pallas kernels, by_kernel(): pl.pallas_call(functools.partial(kernel, n_occ, n_pan, chunks), out_shape...  152 us
    unnamed x3, local copies, waits for them, and re-layouts  32.1 us

profile of v1, /device:TPU:9, one launch (start us, length us, event | category | flops | bytes accessed | tf_op | source)
XLA Modules:
  0.0 189.1 jit_solution(11270210778458622420)
XLA Ops:
  0.0 0.8 dynamic-slice_compare_fusion
  0.8 0.1 eq.57
  0.9 0.8 dynamic_slice.7
  1.7 0.1 eq.58
  1.8 0.6 reduce-window.6
  2.4 0.2 slice_reduce_fusion
  2.7 0.1 add_bitcast_fusion
  2.8 0.2 select_reduce_fusion
  2.9 0.1 copy.14
  3.0 0.1 ne.23
  3.1 0.1 copy.15
  3.2 0.1 rem.19
  3.3 0.1 copy.17
  3.4 0.7 reshape.80.filled_of
  4.0 0.1 copy.16
  4.1 0.1 div.10
  4.2 0.5 and_select_fusion
  4.7 2.3 %copy.19.gamma_ref = bf16[2,256,1088]{2,1,0:T(8,128)(2,1)} copy(bf16[2,256,1088]{1,2,0:T(8,128)(2,1)} %param.5) | data formatting | bytes 2228224 | tf_op args[0]
  7.1 27.5 %copy.18 = bf16[10240,1088]{1,0:T(8,128)(2,1)} copy(bf16[10240,1088]{0,1:T(8,128)(2,1)} %param.6) | data formatting | bytes 44564480 | tf_op args[1]
  34.6 152.2 %shard_map.55 = bf16[8,2,2,128,128]{4,3,2,1,0:T(8,128)(2,1)} custom-call(s32[16]{0:T(128)} %get-tuple-element.10.rows_of, s32[16]{0:T(128)} %get-tuple-element.9.cols_of, s32[16]{0:T(128)} %reshape.80.filled_of, bf16[2,256,1088]{2,1,0:T(8,128)(2,1)} %copy.19.gamma_ref, bf16[4,2,1280,1088]{3,2,1,0:T(8,128)(2,1)} %bitcast.9, bf16[20,128,1024]{2,1,0:T(8,128)(2,1)} %bitcast.10), custom_call_target="tpu_custom_call" | custom-call | tf_op jit(solution)/shard_map/pallas_call | solution.py:301
  186.7 2.3 %copy.21 = bf16[1,1,8,2,2,128,128]{6,5,4,3,2,1,0:T(8,128)(2,1)} copy(bf16[1,1,8,2,2,128,128]{6,5,4,3,2,1,0:T(8,128)(2,1)} %bitcast.11) | data formatting | bytes 2097152
  (8 shorter events, 0.1 us)

commit v2 on v1

v2 whole, which is shorter than its diff:
```python
import functools

import jax
import jax.numpy as jnp
from jax import lax
from jax.experimental import pallas as pl
from jax.experimental.pallas import tpu as pltpu
from jax.sharding import PartitionSpec as P

AUX = 2
TILE = 128
SCAP = 2
PARTS = 5
MESH = pl.DeviceIdType.MESH


def route_slots(block_mask, block_owner, owners):
    usable = block_mask.reshape(-1)
    owners_of = block_owner.reshape(-1)
    belongs = (
        (usable[:, None] == 1)
        & (owners_of[:, None] == jnp.arange(owners, dtype=jnp.int32)[None, :])
    ).astype(jnp.int32)
    order_rank = jnp.cumsum(belongs, axis=0) - belongs
    matched = belongs[:, :, None] * (
        order_rank[:, :, None] == jnp.arange(SCAP, dtype=jnp.int32)[None, None, :]
    ).astype(jnp.int32)
    tile_index = jnp.arange(usable.shape[0], dtype=jnp.int32)
    slot_tile = jnp.sum(matched * tile_index[:, None, None], axis=0)
    filled = jnp.sum(matched, axis=0)
    return (slot_tile, filled)


def block_slots(tile_mask, tile_owner, row_tiles, col_tiles, panels):
    row_block = lax.axis_index("occ")
    col_block = lax.axis_index("pan")
    corner = (row_block * row_tiles, col_block * col_tiles)
    block_mask = lax.dynamic_slice(tile_mask, corner, (row_tiles, col_tiles))
    block_owner = lax.dynamic_slice(tile_owner, corner, (row_tiles, col_tiles))
    return route_slots(block_mask, block_owner, panels)


def by_collectives(gamma_ia, coef_virt, coef_occ, tile_mask, tile_owner):
    panels = lax.axis_size("pan")
    occ_local = gamma_ia.shape[1]
    panel_width = coef_virt.shape[0] // panels
    row_tiles = coef_occ.shape[0] // TILE
    col_tiles = panel_width // TILE
    gamma_flat = gamma_ia.reshape(AUX * occ_local, gamma_ia.shape[2])
    summed = lax.psum_scatter(
        lax.dot_general(
            coef_virt, gamma_flat, (((1,), (1,)), ((), ())), preferred_element_type=jnp.float32
        ),
        "pan",
        scatter_dimension=0,
        tiled=True,
    )
    half_x = summed.astype(jnp.bfloat16).reshape(panel_width, AUX, occ_local)
    whole_x = lax.all_gather(half_x, "occ", axis=2, tiled=True)
    slot_tile, filled = block_slots(tile_mask, tile_owner, row_tiles, col_tiles, panels)
    flat_slots = slot_tile.reshape(-1)
    row_set = jnp.take(
        coef_occ.reshape(row_tiles, TILE, coef_occ.shape[1]), flat_slots // col_tiles, axis=0
    )
    col_set = jnp.take(
        whole_x.reshape(col_tiles, TILE, AUX, whole_x.shape[2]), flat_slots % col_tiles, axis=0
    )
    picked = jnp.einsum("sri,skpi->sprk", row_set, col_set, preferred_element_type=jnp.float32)
    picked = (
        picked.reshape(panels, SCAP, AUX, TILE, TILE)
        * filled.astype(jnp.float32)[:, :, None, None, None]
    )
    arrived = lax.all_to_all(
        picked.astype(jnp.bfloat16), "pan", split_axis=0, concat_axis=0, tiled=True
    )
    return arrived[None, None]


def kernel(
    n_occ, n_pan, parts,
    row_of, col_of, kept_of, gamma_ref, virt_ref, occ_ref, out_ref,
    gamma, virt, coef, send_c, recv_c, keep_a, keep_b, send_a, recv_a, send_b, recv_b,
    keep_2, send_2a, recv_2a, send_2b, recv_2b, whole_0, whole_1, picked,
    load_sem, coef_sem, own_sem,
    c_out, c_in, a_out, a_in, b_out, b_in, a2_out, a2_in, b2_out, b2_in,
    z_out, z_in, t_out, t_in,
):
    o = lax.axis_index("occ")
    s = lax.axis_index("pan")
    core = lax.rem(s, 2)
    x = lax.rem(s // 2, 2)
    y = s // 4
    other_core = s + 1 - 2 * core
    other_x = s + 2 - 4 * x
    other_y = s + 4 - 8 * y
    group = n_pan // 2
    width = virt.shape[3]
    tiles = width // TILE
    half = gamma.shape[1]
    quarter = half // 2
    chunks = AUX * parts
    wholes = (whole_0, whole_1)

    def load(q, pan):
        first = pl.multiple_of(pan * (parts * width) + q * width, width)
        return pltpu.make_async_copy(
            virt_ref.at[:, pl.ds(first, width)], virt.at[q, pan], load_sem.at[q, pan]
        )

    for q in range(parts):
        for g in range(group):
            load(q, 2 * g + 1 - core).start()
        for g in range(group):
            load(q, 2 * g + core).start()
    fetch = pltpu.make_async_copy(occ_ref, coef, coef_sem)
    fetch.start()

    barrier = pltpu.get_barrier_semaphore()
    for d in range(1, n_pan):
        pl.semaphore_signal(
            barrier, inc=1, device_id=(o, lax.rem(s + d, n_pan)), device_id_type=MESH
        )
    for d in range(1, n_occ):
        pl.semaphore_signal(
            barrier, inc=1, device_id=(lax.rem(o + d, n_occ), s), device_id_type=MESH
        )
    for p in range(AUX):
        gamma[p] = gamma_ref[p].T
    pl.semaphore_wait(barrier, n_pan + n_occ - 2)

    def remote(src, dst, out_sem, in_sem, pan, row=None):
        return pltpu.make_async_remote_copy(
            src_ref=src, dst_ref=dst, send_sem=out_sem, recv_sem=in_sem,
            device_id=(o if row is None else row, pan), device_id_type=MESH,
        )

    def copy_c(q):
        return remote(send_c.at[q], recv_c.at[q], c_out.at[q], c_in.at[q], other_core)

    def copy_a(q):
        return remote(send_a.at[q], recv_a.at[q], a_out.at[q], a_in.at[q], other_x)

    def copy_b(q):
        return remote(send_b.at[q], recv_b.at[q], b_out.at[q], b_in.at[q], other_y)

    def copy_2a(q):
        return remote(send_2a.at[q], recv_2a.at[q], a2_out.at[q], a2_in.at[q], other_y)

    def copy_2b(q):
        return remote(send_2b.at[q], recv_2b.at[q], b2_out.at[q], b2_in.at[q], other_x)

    def copy_z(p, q, d, source):
        part = wholes[p].at[source, pl.ds(q * tiles, tiles)]
        return remote(
            part, part, z_out.at[d - 1, p, q], z_in.at[d - 1, p, q], s, lax.rem(o + d, n_occ)
        )

    def product(p, q, pan):
        return lax.dot_general(
            gamma[p],
            virt[q, pan],
            (((1,), (0,)), ((), ())),
            preferred_element_type=jnp.float32,
        )

    def step(it, carry):
        for p in range(AUX):
            @pl.when((it >= 3 + p * parts) & (it < 3 + (p + 1) * parts))
            def _(p=p):
                ch = it - 3
                q = ch - p * parts
                copy_2a(ch).wait_recv()
                copy_2b(ch).wait_recv()
                for h, arrived in ((0, recv_2a), (1, recv_2b)):
                    total = keep_2[h] + arrived[ch].astype(jnp.float32)
                    total = total.astype(jnp.bfloat16)
                    for t in range(tiles):
                        wholes[p][o, q * tiles + t, h * quarter:(h + 1) * quarter] = total[
                            :, t * TILE:(t + 1) * TILE
                        ]
                for d in range(1, n_occ):
                    copy_z(p, q, d, o).start()

        @pl.when((it >= 2) & (it < chunks + 2))
        def _():
            q = it - 2
            copy_a(q).wait_recv()
            send_2a[q] = (keep_a[1] + recv_a[q, 1].astype(jnp.float32)).astype(jnp.bfloat16)
            copy_2a(q).start()
            copy_b(q).wait_recv()
            send_2b[q] = (keep_b[1] + recv_b[q, 1].astype(jnp.float32)).astype(jnp.bfloat16)
            copy_2b(q).start()
            keep_2[0] = keep_a[0] + recv_a[q, 0].astype(jnp.float32)
            keep_2[1] = keep_b[0] + recv_b[q, 0].astype(jnp.float32)

        for p in range(AUX):
            @pl.when((it >= 1 + p * parts) & (it < 1 + (p + 1) * parts))
            def _(p=p):
                ch = it - 1
                q = ch - p * parts
                if p == 0:
                    for g in range(group):
                        load(q, 2 * g + core).wait()
                copy_c(ch).wait_recv()
                for b, a in ((1, 1), (0, 1), (1, 0), (0, 0)):
                    gx = x + a - 2 * x * a
                    gy = y + b - 2 * y * b
                    g = gy * 2 + gx
                    total = product(p, q, 2 * g + core) + recv_c[ch, g].astype(jnp.float32)
                    if a:
                        send_a[ch, b] = total[:quarter].astype(jnp.bfloat16)
                    else:
                        keep_a[b] = total[:quarter]
                    if b:
                        send_b[ch, a] = total[quarter:].astype(jnp.bfloat16)
                    else:
                        keep_b[a] = total[quarter:]
                    if (b, a) == (0, 1):
                        copy_a(ch).start()
                    if (b, a) == (1, 0):
                        copy_b(ch).start()

        for p in range(AUX):
            @pl.when((it >= p * parts) & (it < (p + 1) * parts))
            def _(p=p):
                q = it - p * parts
                if p == 0:
                    for g in range(group):
                        load(q, 2 * g + 1 - core).wait()

                def one(g, c):
                    send_c[it, g] = product(p, q, 2 * g + 1 - core).astype(jnp.bfloat16)
                    return c

                lax.fori_loop(0, group, one, 0)
                copy_c(it).start()

        return carry

    lax.fori_loop(0, chunks + 3, step, 0)

    fetch.wait()

    def tile_send(p, d, source, target):
        return remote(
            picked.at[p, target], out_ref.at[source, p],
            t_out.at[p, d - 1], t_in.at[p, d - 1], target,
        )

    def own(p):
        return pltpu.make_async_copy(picked.at[p, s], out_ref.at[s, p], own_sem.at[p])

    for p in range(AUX):
        for d in range(1, n_occ):
            def arrive(q, c, d=d):
                copy_z(p, q, d, lax.rem(o + n_occ - d, n_occ)).wait_recv()
                return c
            lax.fori_loop(0, parts, arrive, 0)

        def one_owner(d, c):
            j = lax.rem(s + d, n_pan)
            for k in range(SCAP):
                row = row_of[j * SCAP + k]
                col = col_of[j * SCAP + k]
                kept = kept_of[j * SCAP + k].astype(jnp.float32)
                total = lax.dot_general(
                    coef[row],
                    jnp.concatenate(
                        [wholes[p][z, col] for z in range(n_occ)]
                    ),
                    (((1,), (0,)), ((), ())),
                    preferred_element_type=jnp.float32,
                )
                picked[p, j, k] = (total * kept).astype(jnp.bfloat16)

            @pl.when(d < n_pan)
            def _():
                tile_send(p, d, s, j).start()

            return c

        lax.fori_loop(1, n_pan + 1, one_owner, 0)
        own(p).start()

    def drain(ch, c):
        for copy in (copy_c, copy_a, copy_b, copy_2a, copy_2b):
            copy(ch).wait_send()
        return c

    lax.fori_loop(0, chunks, drain, 0)

    for p in range(AUX):
        def drain_z(q, c):
            for d in range(1, n_occ):
                copy_z(p, q, d, o).wait_send()
            return c

        lax.fori_loop(0, parts, drain_z, 0)

        def finish(d, c):
            tile_send(p, d, s, lax.rem(s + d, n_pan)).wait_send()
            source = lax.rem(s + n_pan - d, n_pan)
            tile_send(p, d, source, source).wait_recv()
            return c

        lax.fori_loop(1, n_pan, finish, 0)
        own(p).wait()


def by_kernel(n_occ, n_pan, gamma_ia, coef_virt, coef_occ, tile_mask, tile_owner):
    half = gamma_ia.shape[1]
    depth = gamma_ia.shape[2]
    panel_width = coef_virt.shape[0] // n_pan
    row_tiles = coef_occ.shape[0] // TILE
    col_tiles = panel_width // TILE
    parts = PARTS if col_tiles % PARTS == 0 else 1
    width = panel_width // parts
    chunks = AUX * parts
    group = n_pan // 2
    quarter = half // 2
    slot_tile, filled = block_slots(tile_mask, tile_owner, row_tiles, col_tiles, n_pan)
    flat_slots = slot_tile.reshape(-1)
    bf16, f32 = jnp.bfloat16, jnp.float32
    dma = pltpu.SemaphoreType.DMA
    smem = pl.BlockSpec(memory_space=pltpu.SMEM)
    hbm = pl.BlockSpec(memory_space=pl.ANY)
    arrived = pl.pallas_call(
        functools.partial(kernel, n_occ, n_pan, parts),
        out_shape=jax.ShapeDtypeStruct((n_pan, AUX, SCAP, TILE, TILE), bf16),
        in_specs=[smem, smem, smem, pl.BlockSpec(memory_space=pltpu.VMEM), hbm, hbm],
        out_specs=hbm,
        scratch_shapes=[
            pltpu.VMEM((AUX, half, depth), bf16),
            pltpu.VMEM((parts, n_pan, depth, width), bf16),
            pltpu.VMEM((row_tiles, TILE, coef_occ.shape[1]), bf16),
            pltpu.VMEM((chunks, group, half, width), bf16),
            pltpu.VMEM((chunks, group, half, width), bf16),
            pltpu.VMEM((2, quarter, width), f32),
            pltpu.VMEM((2, quarter, width), f32),
            pltpu.VMEM((chunks, 2, quarter, width), bf16),
            pltpu.VMEM((chunks, 2, quarter, width), bf16),
            pltpu.VMEM((chunks, 2, quarter, width), bf16),
            pltpu.VMEM((chunks, 2, quarter, width), bf16),
            pltpu.VMEM((2, quarter, width), f32),
            pltpu.VMEM((chunks, quarter, width), bf16),
            pltpu.VMEM((chunks, quarter, width), bf16),
            pltpu.VMEM((chunks, quarter, width), bf16),
            pltpu.VMEM((chunks, quarter, width), bf16),
            pltpu.VMEM((n_occ, col_tiles, half, TILE), bf16),
            pltpu.VMEM((n_occ, col_tiles, half, TILE), bf16),
            pltpu.VMEM((AUX, n_pan, SCAP, TILE, TILE), bf16),
            dma((parts, n_pan)), dma, dma((AUX,)),
            *[dma((chunks,)) for _ in range(10)],
            dma((n_occ - 1, AUX, parts)), dma((n_occ - 1, AUX, parts)),
            dma((AUX, n_pan - 1)), dma((AUX, n_pan - 1)),
        ],
        compiler_params=pltpu.CompilerParams(
            collective_id=0, has_side_effects=True, vmem_limit_bytes=67043328
        ),
    )(
        flat_slots // col_tiles,
        flat_slots % col_tiles,
        filled.reshape(-1),
        jnp.swapaxes(gamma_ia, 1, 2),
        coef_virt.T,
        coef_occ.reshape(row_tiles, TILE, coef_occ.shape[1]),
    )
    return jnp.swapaxes(arrived, 1, 2)[None, None]


def solution(mesh):
    n_occ, n_pan = mesh.shape["occ"], mesh.shape["pan"]
    local = functools.partial(by_kernel, n_occ, n_pan) if n_pan == 8 else by_collectives
    return jax.shard_map(
        local,
        mesh=mesh,
        in_specs=(P(None, "occ", "pan"), P(None, "pan"), P("occ", None), P(), P()),
        out_specs=P("occ", "pan", None, None, None, None, None),
        check_vma=False,
    )
```

time: 190 us -> 147 us (0.77)
  the two profiles are of different devices: /device:TPU:9 before, /device:TPU:1 now
where the time goes in v2:
time: 147 us; the launch traced here: 146 us
  Pallas kernels  139 us (95%)
  local copies, waits for them, and re-layouts  4.72 us (3%)
  other arithmetic  2.29 us (2%)
    pallas_call x1, Pallas kernels, by_kernel(): pl.pallas_call(functools.partial(kernel, n_occ, n_pan, parts), out_shape=...  139 us

profile of v2, /device:TPU:1, one launch (start us, length us, event | category | flops | bytes accessed | tf_op | source)
XLA Modules:
  0.0 145.9 jit_solution(12066535177340250283)
XLA Ops:
  0.0 0.8 dynamic-slice_compare_fusion
  0.8 0.1 eq.57
  0.9 0.8 dynamic_slice.7
  1.7 0.1 eq.58
  1.8 0.6 reduce-window.6
  2.4 0.2 slice_reduce_fusion
  2.7 0.1 add_bitcast_fusion
  2.8 0.2 select_reduce_fusion
  2.9 0.1 copy.12
  3.0 0.1 ne.23
  3.1 0.1 copy.13
  3.2 0.1 rem.19
  3.3 0.1 copy.15
  3.4 0.6 reshape.77.kept_of
  4.0 0.1 copy.14
  4.1 0.1 div.10
  4.1 0.6 and_select_fusion
  4.7 138.8 %shard_map.55 = bf16[8,2,2,128,128]{4,3,2,1,0:T(8,128)(2,1)} custom-call(s32[16]{0:T(128)} %get-tuple-element.10.row_of, s32[16]{0:T(128)} %get-tuple-element.9.col_of, s32[16]{0:T(128)} %reshape.77.kept_of, bf16[2,1088,256]{2,1,0:T(8,128)(2,1)} %bitcast.15, bf16[1088,10240]{1,0:T(8,128)(2,1)} %bitcast.12, bf16[20,128,1024]{2,1,0:T(8,128)(2,1)} %bitcast.13), custom_call_target="tpu_custom_call" | custom-call | tf_op jit(solution)/shard_map/pallas_call | solution.py:327
  143.6 2.3 %copy.16 = bf16[1,1,8,2,2,128,128]{6,5,4,3,2,1,0:T(8,128)(2,1)} copy(bf16[1,1,8,2,2,128,128]{6,5,3,4,2,1,0:T(8,128)(2,1)} %bitcast.14) | data formatting | bytes 2097152 | tf_op jit(solution)/shard_map/broadcast_in_dim | solution.py:368
  (8 shorter events, 0.1 us)

commit v3 on v2

--- a/solution.py
+++ b/solution.py
@@ -149,11 +149,20 @@
     def copy_2b(q):
         return remote(send_2b.at[q], recv_2b.at[q], b2_out.at[q], b2_in.at[q], other_x)
 
-    def copy_z(p, q, d, source):
+    last = n_occ - 1
+
+    def copy_z(p, q, way, hop, source):
         part = wholes[p].at[source, pl.ds(q * tiles, tiles)]
+        target = jnp.clip(o + 1 - 2 * way, 0, last)
         return remote(
-            part, part, z_out.at[d - 1, p, q], z_in.at[d - 1, p, q], s, lax.rem(o + d, n_occ)
-        )
+            part, part, z_out.at[way, hop, p, q], z_in.at[way, hop, p, q], s, target
+        )
+
+    def sends(way, hop):
+        return (o < last) & (o >= hop) if way == 0 else (o > 0) & (o + hop <= last)
+
+    def held(way, hop):
+        return o - hop if way == 0 else o + hop
 
     def product(p, q, pan):
         return lax.dot_general(
@@ -178,8 +187,13 @@
                         wholes[p][o, q * tiles + t, h * quarter:(h + 1) * quarter] = total[
                             :, t * TILE:(t + 1) * TILE
                         ]
-                for d in range(1, n_occ):
-                    copy_z(p, q, d, o).start()
+
+            for way in range(2):
+                @pl.when(
+                    (it >= 3 + p * parts) & (it < 3 + (p + 1) * parts) & sends(way, 0)
+                )
+                def _(p=p, way=way):
+                    copy_z(p, it - 3 - p * parts, way, 0, o).start()
 
         @pl.when((it >= 2) & (it < chunks + 2))
         def _():
@@ -235,9 +249,23 @@
                 lax.fori_loop(0, group, one, 0)
                 copy_c(it).start()
 
+        for hop in range(1, last):
+            lag = 3 + 2 * hop
+            for p in range(AUX):
+                for way in range(2):
+                    @pl.when(
+                        (it >= lag + p * parts)
+                        & (it < lag + (p + 1) * parts)
+                        & sends(way, hop)
+                    )
+                    def _(p=p, way=way, hop=hop, lag=lag):
+                        q = it - lag - p * parts
+                        copy_z(p, q, way, hop - 1, held(way, hop)).wait_recv()
+                        copy_z(p, q, way, hop, held(way, hop)).start()
+
         return carry
 
-    lax.fori_loop(0, chunks + 3, step, 0)
+    lax.fori_loop(0, chunks + 3 + 2 * max(last - 1, 0), step, 0)
 
     fetch.wait()
 
@@ -251,11 +279,15 @@
         return pltpu.make_async_copy(picked.at[p, s], out_ref.at[s, p], own_sem.at[p])
 
     for p in range(AUX):
-        for d in range(1, n_occ):
-            def arrive(q, c, d=d):
-                copy_z(p, q, d, lax.rem(o + n_occ - d, n_occ)).wait_recv()
-                return c
-            lax.fori_loop(0, parts, arrive, 0)
+        for hop in range(1, n_occ):
+            for way, end in ((0, last), (1, 0)):
+                @pl.when(o == end)
+                def _(p=p, hop=hop, way=way):
+                    def arrive(q, c):
+                        copy_z(p, q, way, hop - 1, held(way, hop)).wait_recv()
+                        return c
+
+                    lax.fori_loop(0, parts, arrive, 0)
 
         def one_owner(d, c):
             j = lax.rem(s + d, n_pan)
@@ -290,12 +322,15 @@
     lax.fori_loop(0, chunks, drain, 0)
 
     for p in range(AUX):
-        def drain_z(q, c):
-            for d in range(1, n_occ):
-                copy_z(p, q, d, o).wait_send()
-            return c
-
-        lax.fori_loop(0, parts, drain_z, 0)
+        for hop in range(last):
+            for way in range(2):
+                @pl.when(sends(way, hop))
+                def _(p=p, hop=hop, way=way):
+                    def drain_z(q, c):
+                        copy_z(p, q, way, hop, held(way, hop)).wait_send()
+                        return c
+
+                    lax.fori_loop(0, parts, drain_z, 0)
 
         def finish(d, c):
             tile_send(p, d, s, lax.rem(s + d, n_pan)).wait_send()
@@ -351,7 +386,7 @@
             pltpu.VMEM((AUX, n_pan, SCAP, TILE, TILE), bf16),
             dma((parts, n_pan)), dma, dma((AUX,)),
             *[dma((chunks,)) for _ in range(10)],
-            dma((n_occ - 1, AUX, parts)), dma((n_occ - 1, AUX, parts)),
+            dma((2, n_occ - 1, AUX, parts)), dma((2, n_occ - 1, AUX, parts)),
             dma((AUX, n_pan - 1)), dma((AUX, n_pan - 1)),
         ],
         compiler_params=pltpu.CompilerParams(

time: 147 us -> 129 us (0.88)
  Pallas kernels: 139 us -> 122 us
    pallas_call x1, Pallas kernels: 139 us -> 122 us  [by_kernel(): pl.pallas_call(functools.partial(kernel, n_occ, n_pan, parts), out_shape=...]
where the time goes in v3:
time: 129 us
  Pallas kernels  122 us (95%)
  local copies, waits for them, and re-layouts  4.72 us (4%)
  other arithmetic  2.29 us (2%)
    pallas_call x1, Pallas kernels, by_kernel(): pl.pallas_call(functools.partial(kernel, n_occ, n_pan, parts), out_shape=...  122 us

profile of v3, /device:TPU:1, one launch (start us, length us, event | category | flops | bytes accessed | tf_op | source)
XLA Modules:
  0.0 128.8 jit_solution(2689408837942392211)
XLA Ops:
  0.0 0.8 dynamic-slice_compare_fusion
  0.8 0.1 eq.57
  0.9 0.8 dynamic_slice.7
  1.7 0.1 eq.58
  1.8 0.6 reduce-window.6
  2.4 0.2 slice_reduce_fusion
  2.7 0.1 add_bitcast_fusion
  2.8 0.2 select_reduce_fusion
  2.9 0.1 copy.12
  3.0 0.1 ne.23
  3.1 0.1 copy.13
  3.2 0.1 rem.19
  3.3 0.1 copy.15
  3.4 0.6 reshape.77.kept_of
  4.0 0.1 copy.14
  4.1 0.1 div.10
  4.1 0.6 and_select_fusion
  4.7 121.8 %shard_map.55 = bf16[8,2,2,128,128]{4,3,2,1,0:T(8,128)(2,1)} custom-call(s32[16]{0:T(128)} %get-tuple-element.10.row_of, s32[16]{0:T(128)} %get-tuple-element.9.col_of, s32[16]{0:T(128)} %reshape.77.kept_of, bf16[2,1088,256]{2,1,0:T(8,128)(2,1)} %bitcast.15, bf16[1088,10240]{1,0:T(8,128)(2,1)} %bitcast.12, bf16[20,128,1024]{2,1,0:T(8,128)(2,1)} %bitcast.13), custom_call_target="tpu_custom_call" | custom-call | tf_op jit(solution)/shard_map/pallas_call | solution.py:362
  126.5 2.3 %copy.16 = bf16[1,1,8,2,2,128,128]{6,5,4,3,2,1,0:T(8,128)(2,1)} copy(bf16[1,1,8,2,2,128,128]{6,5,3,4,2,1,0:T(8,128)(2,1)} %bitcast.14) | data formatting | bytes 2097152 | tf_op jit(solution)/shard_map/broadcast_in_dim | solution.py:403
  (8 shorter events, 0.1 us)

commit v4 on v3

--- a/solution.py
+++ b/solution.py
@@ -107,13 +107,14 @@
             virt_ref.at[:, pl.ds(first, width)], virt.at[q, pan], load_sem.at[q, pan]
         )
 
-    for q in range(parts):
+    def load_part(q):
         for g in range(group):
             load(q, 2 * g + 1 - core).start()
         for g in range(group):
             load(q, 2 * g + core).start()
+
+    load_part(0)
     fetch = pltpu.make_async_copy(occ_ref, coef, coef_sem)
-    fetch.start()
 
     barrier = pltpu.get_barrier_semaphore()
     for d in range(1, n_pan):
@@ -173,6 +174,14 @@
         )
 
     def step(it, carry):
+        @pl.when(it + 1 < parts)
+        def _():
+            load_part(it + 1)
+
+        @pl.when(it == parts)
+        def _():
+            fetch.start()
+
         for p in range(AUX):
             @pl.when((it >= 3 + p * parts) & (it < 3 + (p + 1) * parts))
             def _(p=p):

time: 129 us -> 129 us (level)
  no operation moved by 1% of the time
where the time goes in v4:
time: 129 us
  Pallas kernels  122 us (95%)
  local copies, waits for them, and re-layouts  4.72 us (4%)
  other arithmetic  2.29 us (2%)
    pallas_call x1, Pallas kernels, by_kernel(): pl.pallas_call(functools.partial(kernel, n_occ, n_pan, parts), out_shape=...  122 us

profile of v4, /device:TPU:1, one launch (start us, length us, event | category | flops | bytes accessed | tf_op | source)
XLA Modules:
  0.0 128.8 jit_solution(7003779845141137648)
XLA Ops:
  0.0 0.8 dynamic-slice_compare_fusion
  0.8 0.1 eq.57
  0.9 0.8 dynamic_slice.7
  1.7 0.1 eq.58
  1.8 0.6 reduce-window.6
  2.4 0.2 slice_reduce_fusion
  2.7 0.1 add_bitcast_fusion
  2.8 0.2 select_reduce_fusion
  2.9 0.1 copy.12
  3.0 0.1 ne.23
  3.1 0.1 copy.13
  3.2 0.1 rem.19
  3.3 0.1 copy.15
  3.4 0.6 reshape.77.kept_of
  4.0 0.1 copy.14
  4.1 0.1 div.10
  4.1 0.6 and_select_fusion
  4.7 121.7 %shard_map.55 = bf16[8,2,2,128,128]{4,3,2,1,0:T(8,128)(2,1)} custom-call(s32[16]{0:T(128)} %get-tuple-element.10.row_of, s32[16]{0:T(128)} %get-tuple-element.9.col_of, s32[16]{0:T(128)} %reshape.77.kept_of, bf16[2,1088,256]{2,1,0:T(8,128)(2,1)} %bitcast.15, bf16[1088,10240]{1,0:T(8,128)(2,1)} %bitcast.12, bf16[20,128,1024]{2,1,0:T(8,128)(2,1)} %bitcast.13), custom_call_target="tpu_custom_call" | custom-call | tf_op jit(solution)/shard_map/pallas_call | solution.py:371
  126.5 2.3 %copy.16 = bf16[1,1,8,2,2,128,128]{6,5,4,3,2,1,0:T(8,128)(2,1)} copy(bf16[1,1,8,2,2,128,128]{6,5,3,4,2,1,0:T(8,128)(2,1)} %bitcast.14) | data formatting | bytes 2097152 | tf_op jit(solution)/shard_map/broadcast_in_dim | solution.py:412
  (8 shorter events, 0.1 us)
